TPU v7x, 32 devices: a whole 2x2x4 slice. The times are simulated.
32 devices in a mesh: inst: 8 (over z, y), space: 4 (over x, core).
Axes of the slice: x: 2, y: 2, z: 4, core: 2. Of those that a mesh axis runs over, the one named last changes fastest.
Arguments:
- state: float32 [32, 320, 512], P('inst', None, 'space'), may hold values from -6 to 6
- forcing: float32 [32, 320, 512], P('inst', None, 'space'), may hold values from -6 to 6
- flux_jac: float32 [3, 5, 5], replicated, may hold values from -0.875 to 0.875
- jacobi_inv: float32 [32, 320, 320], P('inst'), may hold values from -0.01 to 0.03
- cross_nbr: int32 [4, 64], replicated, may hold values from 0 to 63, as said below
- lower_match: int32 [32, 4, 64], P('inst', 'space'), may hold values from 0 to 63, as said below
Outputs:
- residual: float32 [32, 320, 512], P('inst', None, 'space')
- updated: float32 [32, 320, 512], P('inst', None, 'space')
Inputs may be any that keep to these rules, and one draw needn't show every extreme that they name: `cross_nbr`: the cells form a grid of 8 by 8, periodic in both directions, in an order drawn from the seed; if row 0 names n for cell c then row 1 names c for n, and likewise rows 2 and 3. lower_match[t, p] is the identity except at the sliding interface p = 4 // 2, where it is the cyclic pitch shift of the cross_nbr grid by (t * 8 // 32 + r) % 8 rows, with one offset r drawn from the seed: the cell below that faces c is the one reached from c by that many steps through row 1 of cross_nbr.
All inputs are finite; a program needn't handle non-finite values.
Results may differ from a plain program's by a relative error of at most 0.0003.
Values sent between devices are 32-bit elements; how exact they have to be, the bound alone decides.
A program may use at most 128 MiB of HBM per device.

v0:
```python
import math
import jax
import jax.numpy as jnp
import numpy as np
from jax import lax
from jax.sharding import PartitionSpec as P

VARS = 5
NODE1 = 4
PITCH_ELEMENTS = 8
EZ = 8
SWEEPS = 2
dissipation = 0.6
frequency = 0.25


def with_halo(block, sides, width):
    for axis, dim in sides:
        count = lax.axis_size(axis)
        forward = [(i, i + 1) for i in range(count - 1)]
        backward = [(target, source) for source, target in forward]
        low = lax.ppermute(
            lax.slice_in_dim(block, block.shape[dim] - width, None, axis=dim), axis, forward
        )
        high = lax.ppermute(lax.slice_in_dim(block, 0, width, axis=dim), axis, backward)
        block = jnp.concatenate([low, block, high], axis=dim)
    return block


def lobatto_derivative(count_of_nodes):
    inner_point = math.sqrt(0.2)
    points = np.array([-1.0, -inner_point, inner_point, 1.0])
    barycentric = np.ones(count_of_nodes)
    for first_index in range(count_of_nodes):
        for second_index in range(count_of_nodes):
            if first_index != second_index:
                barycentric[first_index] = barycentric[first_index] / (
                    points[first_index] - points[second_index]
                )
    table = np.zeros((count_of_nodes, count_of_nodes))
    for first_index in range(count_of_nodes):
        for second_index in range(count_of_nodes):
            if first_index != second_index:
                table[first_index, second_index] = (
                    barycentric[second_index]
                    / barycentric[first_index]
                    / (points[first_index] - points[second_index])
                )
        table[first_index, first_index] = -np.sum(table[first_index])
    return table


def time_matrix(count):
    pitch_offset = (
        jnp.arange(count, dtype=jnp.int32)[:, None] - jnp.arange(count, dtype=jnp.int32)[None, :]
    )
    parity = 1.0 - 2.0 * (pitch_offset % 2).astype(jnp.float32)
    angle = jnp.pi * pitch_offset.astype(jnp.float32) / count
    safe_tan = jnp.where(pitch_offset == 0, 1.0, jnp.tan(angle))
    return jnp.where(pitch_offset == 0, 0.0, 0.5 * frequency * parity / safe_tan)


def differentiate(stack):
    matrix = time_matrix(stack.shape[0])
    return jnp.einsum("ts,sbe->tbe", matrix, stack, precision=lax.Precision.HIGHEST)


def time_rates(field):
    return lax.all_to_all(
        differentiate(lax.all_to_all(field, "inst", split_axis=2, concat_axis=0, tiled=True)),
        "inst",
        split_axis=0,
        concat_axis=2,
        tiled=True,
    )


def permute_cells(values, index):
    return jnp.take_along_axis(values, index[:, None, :], axis=2)


def face_term(plus, minus, jacobian, sign):
    matrix = sign * jacobian - dissipation * jnp.eye(jacobian.shape[0], dtype=jnp.float32)
    return jnp.einsum("wv,tvabe->twabe", matrix, plus - minus, precision=lax.Precision.HIGHEST)


def space_residual(field, flux_jac, derivative, neighbours, matching_cells, inverse_cells):
    local_times, block, elements = field.shape
    nodes = NODE1
    width = VARS
    cells = PITCH_ELEMENTS * EZ
    face_size = width * nodes * nodes
    highest = lax.Precision.HIGHEST
    reshaped_array = field.reshape(local_times, width, nodes, nodes, nodes, elements)
    low_x = reshaped_array[:, :, 0]
    high_x = reshaped_array[:, :, nodes - 1]
    first_trace = low_x[..., :cells].reshape(local_times, face_size, cells)
    last_trace = high_x[..., elements - cells :].reshape(local_times, face_size, cells)
    outgoing = jnp.concatenate([permute_cells(first_trace, inverse_cells), last_trace], axis=2)
    received = with_halo(outgoing, (("space", 2),), cells)
    from_below = received[:, :, :cells]
    from_above = received[:, :, 3 * cells :]
    from_below = permute_cells(from_below, matching_cells).reshape(
        local_times, width, nodes, nodes, cells
    )
    from_above = from_above.reshape(local_times, width, nodes, nodes, cells)
    plus_low_x = jnp.concatenate([from_below, high_x[..., : elements - cells]], axis=4)
    plus_high_x = jnp.concatenate([low_x[..., cells:], from_above], axis=4)
    along_x = jnp.einsum("ai,tvijke->tvajke", derivative, reshaped_array, precision=highest)
    along_y = jnp.einsum("aj,tvijke->tviake", derivative, reshaped_array, precision=highest)
    along_z = jnp.einsum("ak,tvijke->tvijae", derivative, reshaped_array, precision=highest)
    volume = jnp.einsum("wv,tvijke->twijke", flux_jac[0], along_x, precision=highest)
    volume = volume + jnp.einsum("wv,tvijke->twijke", flux_jac[1], along_y, precision=highest)
    volume = volume + jnp.einsum("wv,tvijke->twijke", flux_jac[2], along_z, precision=highest)
    scale = nodes * (nodes - 1) / 4.0
    low_y = reshaped_array[:, :, :, 0]
    high_y = reshaped_array[:, :, :, nodes - 1]
    low_z = reshaped_array[:, :, :, :, 0]
    high_z = reshaped_array[:, :, :, :, nodes - 1]
    volume = volume.at[:, :, 0].add(scale * face_term(plus_low_x, low_x, flux_jac[0], -1.0))
    volume = volume.at[:, :, nodes - 1].add(
        scale * face_term(plus_high_x, high_x, flux_jac[0], 1.0)
    )
    volume = volume.at[:, :, :, 0].add(
        scale * face_term(jnp.take(high_y, neighbours[0], axis=4), low_y, flux_jac[1], -1.0)
    )
    volume = volume.at[:, :, :, nodes - 1].add(
        scale * face_term(jnp.take(low_y, neighbours[1], axis=4), high_y, flux_jac[1], 1.0)
    )
    volume = volume.at[:, :, :, :, 0].add(
        scale * face_term(jnp.take(high_z, neighbours[2], axis=4), low_z, flux_jac[2], -1.0)
    )
    volume = volume.at[:, :, :, :, nodes - 1].add(
        scale * face_term(jnp.take(low_z, neighbours[3], axis=4), high_z, flux_jac[2], 1.0)
    )
    return volume.reshape(local_times, block, elements)


def body(state, forcing, flux_jac, jacobi_inv, cross_nbr, lower_match):
    local_times, block, elements = state.shape
    cells = PITCH_ELEMENTS * EZ
    derivative = jnp.asarray(lobatto_derivative(NODE1), jnp.float32)
    layer_start = jnp.arange(elements // cells, dtype=jnp.int32) * cells
    neighbours = (layer_start[None, :, None] + cross_nbr[:, None, :]).reshape(4, elements)
    matching_cells = lower_match[:, 0, :]
    inverse_cells = jnp.argsort(matching_cells, axis=-1)
    current = state
    first_residual = state
    for sweep in range(SWEEPS):
        rates = time_rates(current)
        spatial = space_residual(
            current, flux_jac, derivative, neighbours, matching_cells, inverse_cells
        )
        residual = spatial + rates - forcing
        if sweep == 0:
            first_residual = residual
        current = current - jnp.einsum(
            "tpq,tqe->tpe", jacobi_inv, residual, precision=lax.Precision.HIGHEST
        )
    return (first_residual, current)


def solution(mesh):
    return jax.shard_map(
        body,
        mesh=mesh,
        in_specs=(
            P("inst", None, "space"),
            P("inst", None, "space"),
            P(),
            P("inst", None, None),
            P(),
            P("inst", "space", None),
        ),
        out_specs=(P("inst", None, "space"), P("inst", None, "space")),
        check_vma=False,
    )
```

profile of v0, /device:TPU:1, one launch (start us, length us, event | category | flops | bytes accessed | tf_op | source)
XLA Modules:
  0.0 344.2 jit_solution(9277258930535717636)
XLA Ops:
  7.5 1.9 collective-permute-start.1
  10.9 4.5 %collective-permute-start = (f32[4,80,64]{1,2,0:T(8,128)}, f32[4,80,64]{1,2,0:T(8,128)S(1)}, u32[]{:S(2)}, u32[]{:S(2)}) collective-permute-start(f32[4,80,64]{1,2,0:T(8,128)} %copy.324), channel_id=1, source_target_pairs={{0,1},{1,2},{2,3},{4,5},{5,6},{6,7},{8,9},{9,10},{10,11},{12,13},{... | collective-permute-start | bytes 245768 | tf_op jit(solution)/shard_map/ppermute | solution.py:22
  16.5 6.1 %all-to-all-start = ((f32[4,320,128]{1,0,2:T(4,128)}), f32[4,320,128]{1,0,2:T(4,128)}, u32[]{:S(2)}, u32[]{:S(2)}) async-start(f32[4,320,128]{1,0,2:T(4,128)} %copy.355), calls=%async_computation | async-start | bytes 1572864 | tf_op jit(solution)/shard_map/all_to_all | solution.py:70
  22.7 2.2 convolution_bitcast_fusion.5
  24.8 2.0 convolution_bitcast_fusion.4
  30.4 4.5 %copy.455 = f32[4,5,4,4,1,128]{1,3,2,0,5,4:T(4,128)} copy(f32[4,5,4,4,1,128]{5,4,3,2,1,0:T(1,128)} %get-tuple-element.160) | data formatting | bytes 327680
  34.9 4.3 %copy.463 = f32[4,5,4,4,1,128]{1,3,5,2,0,4:T(4,128)} copy(f32[4,5,4,4,1,128]{5,4,3,2,1,0:T(1,128)} %get-tuple-element.160) | data formatting | bytes 327680 | tf_op jit(solution)/shard_map/squeeze | solution.py:118
  39.2 2.4 fusion.145
  41.7 2.4 convolution_add_fusion.3
  46.5 4.6 %copy.451 = f32[4,5,4,1,4,128]{1,4,2,0,5,3:T(4,128)} copy(f32[4,5,4,1,4,128]{5,4,3,2,1,0:T(4,128)} %get-tuple-element.162) | data formatting | bytes 327680
  51.1 4.3 %copy.450 = f32[4,5,4,1,4,128]{1,4,5,2,0,3:T(4,128)} copy(f32[4,5,4,1,4,128]{5,4,3,2,1,0:T(4,128)} %get-tuple-element.163) | data formatting | bytes 327680
  55.4 3.2 copy.342
  58.6 3.3 copy.454
  61.9 7.7 %gather_fusion.2 = f32[128,4,5,4,4]{2,4,3,1,0:T(4,128)} fusion(f32[4,5,4,4,128]{1,3,4,2,0:T(4,128)} %bitcast.450, s32[1024]{0:T(1024)S(1)} %pad_clamp_fusion.3), kind=kCustom, calls=%fused_computation.1.clone | custom fusion | bytes 328192 | tf_op jit(solution)/shard_map/jit(_take)/gather | solution.py:125
  69.6 7.7 %gather_fusion.3 = f32[128,4,5,4,4]{2,4,3,1,0:T(4,128)} fusion(f32[4,5,4,4,128]{1,3,4,2,0:T(4,128)} %copy.342, s32[1024]{0:T(1024)S(1)} %pad_clamp_fusion.2), kind=kCustom, calls=%fused_computation.5.clone | custom fusion | bytes 328192 | tf_op jit(solution)/shard_map/jit(_take)/gather | solution.py:128
  77.4 6.0 %bitcast_subtract_fusion.6 = f32[4,5,4,4,128]{1,3,4,2,0:T(4,128)} fusion(f32[128,4,5,4,4]{2,4,3,1,0:T(4,128)} %gather_fusion.3, pred[128]{0:T(512)(128)(4,1)S(1)} %get-tuple-element.189, f32[4,5,4,1,4,128]{1,4,5,2,0,3:T(4,128)} %copy.450), kind=kLoop, calls=%fused_computation.22 | loop fusion | flops 81920 | bytes 491648 | tf_op jit(solution)/shard_map/sub | solution.py:84
  83.3 7.8 %gather_fusion.4 = f32[128,4,5,4,4]{2,4,3,1,0:T(4,128)} fusion(f32[4,5,4,4,128]{1,3,4,2,0:T(4,128)} %bitcast.451, s32[1024]{0:T(1024)S(1)} %pad_clamp_fusion.1), kind=kCustom, calls=%fused_computation.6.clone | custom fusion | bytes 328192 | tf_op jit(solution)/shard_map/jit(_take)/gather | solution.py:131
  91.1 7.7 %gather_fusion.5 = f32[128,4,5,4,4]{2,4,3,1,0:T(4,128)} fusion(f32[4,5,4,4,128]{1,3,4,2,0:T(4,128)} %bitcast.455, s32[1024]{0:T(1024)S(1)} %pad_clamp_fusion), kind=kCustom, calls=%fused_computation.7.clone | custom fusion | bytes 328192 | tf_op jit(solution)/shard_map/jit(_take)/gather | solution.py:134
  98.8 5.9 %bitcast_subtract_fusion.4 = f32[4,5,4,4,128]{1,3,4,2,0:T(4,128)} fusion(f32[128,4,5,4,4]{2,4,3,1,0:T(4,128)} %gather_fusion.5, pred[128]{0:T(512)(128)(4,1)S(1)} %get-tuple-element.187, f32[4,5,4,4,1,128]{1,3,5,2,0,4:T(4,128)} %copy.454), kind=kLoop, calls=%fused_computation.20 | loop fusion | flops 81920 | bytes 491648 | tf_op jit(solution)/shard_map/sub | solution.py:84
  106.3 3.1 bitcast_subtract_fusion.7
  111.3 3.5 %bitcast_subtract_fusion.5 = f32[4,5,4,4,128]{1,3,2,0,4:T(4,128)} fusion(f32[4,5,4,4,1,128]{1,3,2,0,5,4:T(4,128)S(1)} %copy-done.7, f32[128,4,5,4,4]{2,4,3,1,0:T(4,128)S(1)} %copy-done.13, pred[128]{0:T(512)(128)(4,1)S(1)} %get-tuple-element.188), kind=kLoop, calls=%fused_computation.21 | loop fusion | flops 81920 | bytes 491648 | tf_op jit(solution)/shard_map/sub | solution.py:84
  124.3 6.9 %fusion.126 = f32[4,5,4,4,4,128]{5,1,4,3,2,0:T(8,128)} fusion(f32[4,5,4,4,4,128]{5,1,4,3,2,0:T(8,128)} %fusion.134, f32[4,5,4,1,4,128]{5,1,4,2,0,3:T(8,128)S(1)} %slice_bitcast_fusion.2, f32[4,5,4,4,128]{1,3,2,0,4:T(4,128)S(1)} %copy-done.8, f32[1,5,5]{2,0,1:T(1,128)S(1)} %get-tuple-element.177), kind=kOutput, calls=%fused_computation.98 | convolution fusion | flops 2539620 | bytes 589924 | tf_op jit(solution)/shard_map/wv,tvabe->twabe/dot_general | solution.py:84
  135.7 2.0 fusion.175
  139.1 5.6 %all-to-all-start.1 = ((f32[32,320,16]{1,2,0:T(8,128)}), f32[32,320,16]{1,2,0:T(8,128)S(1)}, u32[]{:S(2)}, u32[]{:S(2)}) async-start(f32[32,320,16]{1,2,0:T(8,128)} %copy.358), calls=%async_computation.1 | async-start | bytes 1572864 | tf_op jit(solution)/shard_map/all_to_all | solution.py:69
  144.7 6.8 %fusion.117 = f32[4,5,4,4,4,128]{5,1,4,3,2,0:T(8,128)} fusion(f32[4,5,4,4,4,128]{5,1,4,3,2,0:T(8,128)} %fusion.126, f32[4,5,4,1,4,128]{5,1,4,2,0,3:T(8,128)} %slice_bitcast_fusion.1, f32[4,5,4,4,128]{1,3,4,2,0:T(4,128)} %bitcast_subtract_fusion.6, f32[1,5,5]{2,0,1:T(1,128)S(1)} %get-tuple-element.177), kind=kOutput, calls=%fused_computation.95 | convolution fusion | flops 2539595 | bytes 4718692 | tf_op jit(solution)/shard_map/wv,tvabe->twabe/dot_general | solution.py:84
  152.5 8.9 %fusion.108 = f32[4,5,4,4,4,128]{5,1,4,3,2,0:T(8,128)} fusion(f32[4,5,4,4,4,128]{5,1,4,3,2,0:T(8,128)} %fusion.117, f32[4,5,4,4,1,128]{5,1,3,2,0,4:T(8,128)S(1)} %slice_bitcast_fusion, f32[4,5,4,4,128]{1,3,2,0,4:T(4,128)} %bitcast_subtract_fusion.5, f32[1,5,5]{2,0,1:T(1,128)S(1)} %get-tuple-element.176), kind=kOutput, calls=%fused_computation.92 | convolution fusion | flops 2539620 | bytes 4620388 | tf_op jit(solution)/shard_map/wv,tvabe->twabe/dot_general | solution.py:84
  161.4 5.6 %fusion.99 = f32[4,5,4,4,4,128]{5,1,4,3,2,0:T(8,128)} fusion(f32[4,5,4,4,4,128]{5,1,4,3,2,0:T(8,128)} %fusion.108, f32[4,5,4,4,128]{1,3,4,2,0:T(4,128)S(1)} %copy-done.4, f32[1,5,5]{2,0,1:T(1,128)S(1)} %get-tuple-element.176), kind=kOutput, calls=%fused_computation.89 | convolution fusion | flops 2539595 | bytes 688228 | tf_op jit(solution)/shard_map/wv,tvabe->twabe/dot_general | solution.py:84
  167.0 2.2 copy.354
  173.1 1.9 fusion.19
  176.3 2.1 convolution_bitcast_fusion.1
  178.4 2.1 convolution_bitcast_fusion
  183.0 3.4 copy.461
  186.4 3.2 copy.465
  190.8 2.3 fusion.141
  199.3 2.1 collective-permute-start.3
  202.3 3.7 %collective-permute-start.2 = (f32[4,80,64]{1,2,0:T(8,128)S(1)}, f32[4,80,64]{1,2,0:T(8,128)S(1)}, u32[]{:S(2)}, u32[]{:S(2)}) collective-permute-start(f32[4,80,64]{1,2,0:T(8,128)S(1)} %copy.370), channel_id=1, source_target_pairs={{0,1},{1,2},{2,3},{4,5},{5,6},{6,7},{8,9},{9,10},{10,11},{12,13},{... | collective-permute-start | bytes 245768 | tf_op jit(solution)/shard_map/ppermute | solution.py:22
  206.0 3.8 %copy.459 = f32[4,5,4,1,4,128]{1,4,2,0,5,3:T(4,128)} copy(f32[4,5,4,1,4,128]{5,4,3,2,1,0:T(4,128)S(1)} %copy-done.23) | data formatting | bytes 327680
  209.8 3.2 copy.458
  212.9 7.7 %gather_fusion.8 = f32[128,4,5,4,4]{2,4,3,1,0:T(4,128)} fusion(f32[4,5,4,4,128]{1,3,4,2,0:T(4,128)} %bitcast.452, s32[1024]{0:T(1024)S(1)} %pad_clamp_fusion.3), kind=kCustom, calls=%fused_computation.8.clone | custom fusion | bytes 328192 | tf_op jit(solution)/shard_map/jit(_take)/gather | solution.py:125
  220.7 3.1 copy.386
  223.8 7.8 %gather_fusion.9 = f32[128,4,5,4,4]{2,4,3,1,0:T(4,128)} fusion(f32[4,5,4,4,128]{1,3,4,2,0:T(4,128)} %copy.386, s32[1024]{0:T(1024)S(1)} %pad_clamp_fusion.2), kind=kCustom, calls=%fused_computation.9.clone | custom fusion | bytes 328192 | tf_op jit(solution)/shard_map/jit(_take)/gather | solution.py:128
  231.5 5.8 %bitcast_subtract_fusion.2 = f32[4,5,4,4,128]{1,3,4,2,0:T(4,128)} fusion(f32[128,4,5,4,4]{2,4,3,1,0:T(4,128)} %gather_fusion.9, pred[128]{0:T(512)(128)(4,1)S(1)} %get-tuple-element.189, f32[4,5,4,1,4,128]{1,4,5,2,0,3:T(4,128)} %copy.458), kind=kLoop, calls=%fused_computation.16 | loop fusion | flops 81920 | bytes 491648 | tf_op jit(solution)/shard_map/sub | solution.py:84
  237.3 3.3 copy.460
  240.6 7.8 %gather_fusion.10 = f32[128,4,5,4,4]{2,4,3,1,0:T(4,128)} fusion(f32[4,5,4,4,128]{1,3,4,2,0:T(4,128)} %bitcast.453, s32[1024]{0:T(1024)S(1)} %pad_clamp_fusion.1), kind=kCustom, calls=%fused_computation.10.clone | custom fusion | bytes 328192 | tf_op jit(solution)/shard_map/jit(_take)/gather | solution.py:131
  248.4 7.7 %gather_fusion.11 = f32[128,4,5,4,4]{2,4,3,1,0:T(4,128)} fusion(f32[4,5,4,4,128]{1,3,4,2,0:T(4,128)} %bitcast.454, s32[1024]{0:T(1024)S(1)} %pad_clamp_fusion), kind=kCustom, calls=%fused_computation.11.clone | custom fusion | bytes 328192 | tf_op jit(solution)/shard_map/jit(_take)/gather | solution.py:134
  256.1 5.8 %bitcast_subtract_fusion = f32[4,5,4,4,128]{1,3,4,2,0:T(4,128)} fusion(f32[128,4,5,4,4]{2,4,3,1,0:T(4,128)} %gather_fusion.11, pred[128]{0:T(512)(128)(4,1)S(1)} %get-tuple-element.187, f32[4,5,4,4,1,128]{1,3,5,2,0,4:T(4,128)} %copy.460), kind=kLoop, calls=%fused_computation.12 | loop fusion | flops 81920 | bytes 491648 | tf_op jit(solution)/shard_map/sub | solution.py:84
  261.9 6.0 %all-to-all-start.2 = ((f32[4,320,128]{1,0,2:T(4,128)}), f32[4,320,128]{1,0,2:T(4,128)}, u32[]{:S(2)}, u32[]{:S(2)}) async-start(f32[4,320,128]{1,0,2:T(4,128)} %copy.398), calls=%async_computation.2 | async-start | bytes 1572864 | tf_op jit(solution)/shard_map/all_to_all | solution.py:70
  267.9 2.8 convolution_add_fusion.1
  270.7 5.8 %bitcast_subtract_fusion.3 = f32[4,5,4,4,128]{1,3,2,0,4:T(4,128)} fusion(f32[4,5,4,1,4,128]{1,4,2,0,5,3:T(4,128)} %copy.459, f32[128,4,5,4,4]{2,4,3,1,0:T(4,128)} %gather_fusion.8, pred[128]{0:T(512)(128)(4,1)S(1)} %get-tuple-element.190), kind=kLoop, calls=%fused_computation.19 | loop fusion | flops 81920 | bytes 491648 | tf_op jit(solution)/shard_map/sub | solution.py:84
  278.1 3.1 bitcast_subtract_fusion.1
  281.2 2.4 fusion.16
  286.9 2.1 fusion.136
  289.0 2.1 fusion.138
  293.6 2.3 all_to_all.63
  295.9 2.0 fusion.173
  299.2 5.8 %all-to-all-start.3 = ((f32[32,320,16]{1,2,0:T(8,128)}), f32[32,320,16]{1,2,0:T(8,128)}, u32[]{:S(2)}, u32[]{:S(2)}) async-start(f32[32,320,16]{1,2,0:T(8,128)} %copy.401), calls=%async_computation.3 | async-start | bytes 1572864 | tf_op jit(solution)/shard_map/all_to_all | solution.py:69
  305.1 9.1 %fusion.81 = f32[4,5,4,4,4,128]{5,1,3,2,0,4:T(8,128)} fusion(f32[4,5,4,4,4,128]{5,1,3,2,0,4:T(8,128)} %fusion.138, f32[4,5,4,4,128]{1,3,2,0,4:T(4,128)} %bitcast_subtract_fusion.3, f32[1,5,5]{2,0,1:T(1,128)S(1)} %get-tuple-element.177), kind=kOutput, calls=%fused_computation.83 | convolution fusion | flops 2539620 | bytes 4718692 | tf_op jit(solution)/shard_map/wv,tvabe->twabe/dot_general | solution.py:84
  314.2 5.6 %fusion.75 = f32[4,5,4,4,4,128]{5,1,3,2,0,4:T(8,128)} fusion(f32[4,5,4,4,4,128]{5,1,3,2,0,4:T(8,128)} %fusion.81, f32[4,5,4,4,128]{1,3,4,2,0:T(4,128)S(1)} %copy-done.2, f32[1,5,5]{2,0,1:T(1,128)S(1)} %get-tuple-element.177), kind=kOutput, calls=%fused_computation.81 | convolution fusion | flops 2539595 | bytes 688228 | tf_op jit(solution)/shard_map/wv,tvabe->twabe/dot_general | solution.py:84
  319.8 7.9 %fusion.93 = f32[4,5,4,4,4,128]{5,1,3,2,0,4:T(8,128)} fusion(f32[4,5,4,4,4,128]{5,1,3,2,0,4:T(8,128)} %fusion.75, f32[4,5,4,4,128]{1,3,2,0,4:T(4,128)S(1)} %copy-done.6, f32[1,5,5]{2,0,1:T(1,128)S(1)} %get-tuple-element.176), kind=kOutput, calls=%fused_computation.87 | convolution fusion | flops 2539620 | bytes 688228 | tf_op jit(solution)/shard_map/wv,tvabe->twabe/dot_general | solution.py:84
  327.7 5.5 %fusion.87 = f32[4,5,4,4,4,128]{5,1,3,2,0,4:T(8,128)} fusion(f32[4,5,4,4,4,128]{5,1,3,2,0,4:T(8,128)} %fusion.93, f32[4,5,4,4,128]{1,3,4,2,0:T(4,128)S(1)} %copy-done.3, f32[1,5,5]{2,0,1:T(1,128)S(1)} %get-tuple-element.176), kind=kOutput, calls=%fused_computation.85 | convolution fusion | flops 2539595 | bytes 688228 | tf_op jit(solution)/shard_map/wv,tvabe->twabe/dot_general | solution.py:84
  333.2 2.5 copy.397
  335.7 2.1 copy.402
  337.8 2.2 copy.403
  340.0 4.0 %fusion.18 = f32[4,320,128]{2,1,0:T(8,128)} fusion(f32[4,320,128]{2,1,0:T(8,128)S(1)} %fusion.19, f32[4,320,320]{2,1,0:T(8,128)S(1)} %copy-done, f32[4,320,128]{2,1,0:T(8,128)S(1)} %copy-done.15, f32[4,320,128]{2,1,0:T(8,128)} %bitcast.461, f32[4,320,128]{2,1,0:T(8,128)} %copy.403), kind=kOutput, calls=%fused_computation.53 | convolution fusion | flops 629637120 | bytes 4915200 | tf_op jit(solution)/shard_map/tpq,tqe->tpe/dot_general | solution.py:157
  (150 shorter events, 59.6 us)
Async XLA Ops:
  0.6 172.4 %copy-start = (f32[4,320,320]{2,1,0:T(8,128)S(1)}, f32[4,320,320]{2,1,0:T(8,128)}, u32[]{:S(2)}) copy-start(f32[4,320,320]{2,1,0:T(8,128)} %param.38) | copy-start | bytes 4915204
  0.6 22.0 %copy-start.28 = (f32[4,4,1,1,1,1]{1,0,5,4,3,2:T(4,128)S(1)}, f32[4,4,1,1,1,1]{1,0,5,4,3,2:T(4,128)}, u32[]{:S(2)}) copy-start(f32[4,4,1,1,1,1]{1,0,5,4,3,2:T(4,128)} %constant.421) | copy-start | bytes 196
  0.7 14.7 %copy-start.1 = (f32[4,320,128]{2,1,0:T(8,128)S(1)}, f32[4,320,128]{2,1,0:T(8,128)}, u32[]{:S(2)}) copy-start(f32[4,320,128]{2,1,0:T(8,128)} %param.35) | copy-start | bytes 1966084
  6.7 21.4 %copy-start.29 = (s32[4,1,64]{2,1,0:T(1,128)S(1)}, s32[4,1,64]{2,1,0:T(1,128)}, u32[]{:S(2)}) copy-start(s32[4,1,64]{2,1,0:T(1,128)} %param.40) | copy-start | bytes 3076
  7.5 111.2 %collective-permute-start.1 = (f32[4,80,64]{2,1,0:T(8,128)}, f32[4,80,64]{2,1,0:T(8,128)}, u32[]{:S(2)}, u32[]{:S(2)}) collective-permute-start(f32[4,80,64]{2,1,0:T(8,128)} %select_bitcast_fusion.1), channel_id=1, source_target_pairs={{1,0},{2,1},{3,2},{5,4},{6,5},{7,6},{9,8},{10,9},{11,10},{13,12},{... | collective-permute-start | bytes 245768 | tf_op jit(solution)/shard_map/ppermute | solution.py:25
  10.1 18.8 %copy-start.31 = (s32[4,64]{1,0:T(4,128)S(1)}, s32[4,64]{1,0:T(4,128)}, u32[]{:S(2)}) copy-start(s32[4,64]{1,0:T(4,128)} %param.39) | copy-start | bytes 3076
  10.9 104.0 %collective-permute-start = (f32[4,80,64]{1,2,0:T(8,128)}, f32[4,80,64]{1,2,0:T(8,128)S(1)}, u32[]{:S(2)}, u32[]{:S(2)}) collective-permute-start(f32[4,80,64]{1,2,0:T(8,128)} %copy.324), channel_id=1, source_target_pairs={{0,1},{1,2},{2,3},{4,5},{5,6},{6,7},{8,9},{9,10},{10,11},{12,13},{... | collective-permute-start | bytes 245768 | tf_op jit(solution)/shard_map/ppermute | solution.py:22
  16.5 116.3 %all-to-all-start = ((f32[4,320,128]{1,0,2:T(4,128)}), f32[4,320,128]{1,0,2:T(4,128)}, u32[]{:S(2)}, u32[]{:S(2)}) async-start(f32[4,320,128]{1,0,2:T(4,128)} %copy.355), calls=%async_computation | async-start | bytes 1572864 | tf_op jit(solution)/shard_map/all_to_all | solution.py:70
  30.4 8.8 %copy-start.30 = (f32[3,5,5]{2,0,1:T(4,128)S(1)}, f32[3,5,5]{2,0,1:T(4,128)}, u32[]{:S(2)}) copy-start(f32[3,5,5]{2,0,1:T(4,128)} %param.37) | copy-start | bytes 904
  45.5 1.0 copy-start.10
  46.5 8.9 %copy-start.20 = (f32[4,5,4,4,128]{4,3,2,1,0:T(4,128)S(1)}, f32[4,5,4,4,128]{4,3,2,1,0:T(4,128)}, u32[]{:S(2)}) copy-start(f32[4,5,4,4,128]{4,3,2,1,0:T(4,128)} %get-tuple-element.161) | copy-start | bytes 491524
  51.1 7.5 %copy-start.19 = (f32[4,5,4,4,1,128]{5,4,3,2,1,0:T(1,128)S(1)}, f32[4,5,4,4,1,128]{5,4,3,2,1,0:T(1,128)}, u32[]{:S(2)}) copy-start(f32[4,5,4,4,1,128]{5,4,3,2,1,0:T(1,128)} %get-tuple-element.159) | copy-start | bytes 491524
  98.8 5.9 %copy-start.9 = (f32[4,5,4,1,4,128]{1,4,2,0,5,3:T(4,128)S(1)}, f32[4,5,4,1,4,128]{1,4,2,0,5,3:T(4,128)}, u32[]{:S(2)}) copy-start(f32[4,5,4,1,4,128]{1,4,2,0,5,3:T(4,128)} %copy.451) | copy-start | bytes 491524
  98.8 7.4 %copy-start.12 = (f32[128,4,5,4,4]{2,4,3,1,0:T(4,128)S(1)}, f32[128,4,5,4,4]{2,4,3,1,0:T(4,128)}, u32[]{:S(2)}) copy-start(f32[128,4,5,4,4]{2,4,3,1,0:T(4,128)} %gather_fusion.2) | copy-start | bytes 491524
  106.3 3.1 copy-start.7
  106.3 5.0 %copy-start.13 = (f32[128,4,5,4,4]{2,4,3,1,0:T(4,128)S(1)}, f32[128,4,5,4,4]{2,4,3,1,0:T(4,128)}, u32[]{:S(2)}) copy-start(f32[128,4,5,4,4]{2,4,3,1,0:T(4,128)} %gather_fusion.4) | copy-start | bytes 491524
  111.3 7.4 %copy-start.24 = (f32[4,5,1,4,4,64]{5,4,3,1,0,2:T(4,128)S(1)}, f32[4,5,1,4,4,64]{5,4,3,1,0,2:T(4,128)}, u32[]{:S(2)}) copy-start(f32[4,5,1,4,4,64]{5,4,3,1,0,2:T(4,128)} %get-tuple-element.172) | copy-start | bytes 245764
  111.3 7.4 %copy-start.25 = (f32[4,5,1,4,4,64]{5,4,3,1,0,2:T(4,128)S(1)}, f32[4,5,1,4,4,64]{5,4,3,1,0,2:T(4,128)}, u32[]{:S(2)}) copy-start(f32[4,5,1,4,4,64]{5,4,3,1,0,2:T(4,128)} %get-tuple-element.175) | copy-start | bytes 245764
  117.5 6.7 %copy-start.8 = (f32[4,5,4,4,128]{1,3,2,0,4:T(4,128)S(1)}, f32[4,5,4,4,128]{1,3,2,0,4:T(4,128)}, u32[]{:S(2)}) copy-start(f32[4,5,4,4,128]{1,3,2,0,4:T(4,128)} %bitcast_subtract_fusion.7) | copy-start | bytes 491524
  139.1 30.2 %all-to-all-start.1 = ((f32[32,320,16]{1,2,0:T(8,128)}), f32[32,320,16]{1,2,0:T(8,128)S(1)}, u32[]{:S(2)}, u32[]{:S(2)}) async-start(f32[32,320,16]{1,2,0:T(8,128)} %copy.358), calls=%async_computation.1 | async-start | bytes 1572864 | tf_op jit(solution)/shard_map/all_to_all | solution.py:69
  144.7 16.7 %copy-start.4 = (f32[4,5,4,4,128]{1,3,4,2,0:T(4,128)S(1)}, f32[4,5,4,4,128]{1,3,4,2,0:T(4,128)}, u32[]{:S(2)}) copy-start(f32[4,5,4,4,128]{1,3,4,2,0:T(4,128)} %bitcast_subtract_fusion.4) | copy-start | bytes 491524
  173.0 8.2 %copy-start.16 = (f32[4,320,128]{2,1,0:T(8,128)}, f32[4,320,128]{2,1,0:T(8,128)S(1)}, u32[]{:S(2)}) copy-start(f32[4,320,128]{2,1,0:T(8,128)S(1)} %add_subtract_fusion) | copy-start | bytes 1966084
  189.6 11.9 %copy-start.17 = (f32[4,5,4,4,128]{4,3,2,1,0:T(4,128)S(1)}, f32[4,5,4,4,128]{4,3,2,1,0:T(4,128)}, u32[]{:S(2)}) copy-start(f32[4,5,4,4,128]{4,3,2,1,0:T(4,128)} %get-tuple-element.158) | copy-start | bytes 491524
  193.1 12.9 %copy-start.23 = (f32[4,5,4,1,4,128]{5,4,3,2,1,0:T(4,128)S(1)}, f32[4,5,4,1,4,128]{5,4,3,2,1,0:T(4,128)}, u32[]{:S(2)}) copy-start(f32[4,5,4,1,4,128]{5,4,3,2,1,0:T(4,128)} %get-tuple-element.153) | copy-start | bytes 491524
  193.1 16.7 %copy-start.22 = (f32[4,5,4,1,4,128]{5,4,3,2,1,0:T(4,128)S(1)}, f32[4,5,4,1,4,128]{5,4,3,2,1,0:T(4,128)}, u32[]{:S(2)}) copy-start(f32[4,5,4,1,4,128]{5,4,3,2,1,0:T(4,128)} %get-tuple-element.154) | copy-start | bytes 491524
  199.3 86.3 %collective-permute-start.3 = (f32[4,80,64]{2,1,0:T(8,128)}, f32[4,80,64]{2,1,0:T(8,128)}, u32[]{:S(2)}, u32[]{:S(2)}) collective-permute-start(f32[4,80,64]{2,1,0:T(8,128)} %select_bitcast_fusion), channel_id=1, source_target_pairs={{1,0},{2,1},{3,2},{5,4},{6,5},{7,6},{9,8},{10,9},{11,10},{13,12},{... | collective-permute-start | bytes 245768 | tf_op jit(solution)/shard_map/ppermute | solution.py:25
  202.3 81.3 %collective-permute-start.2 = (f32[4,80,64]{1,2,0:T(8,128)S(1)}, f32[4,80,64]{1,2,0:T(8,128)S(1)}, u32[]{:S(2)}, u32[]{:S(2)}) collective-permute-start(f32[4,80,64]{1,2,0:T(8,128)S(1)} %copy.370), channel_id=1, source_target_pairs={{0,1},{1,2},{2,3},{4,5},{5,6},{6,7},{8,9},{9,10},{10,11},{12,13},{... | collective-permute-start | bytes 245768 | tf_op jit(solution)/shard_map/ppermute | solution.py:22
  206.0 14.7 %copy-start.21 = (f32[4,5,4,4,128]{4,3,2,1,0:T(4,128)S(1)}, f32[4,5,4,4,128]{4,3,2,1,0:T(4,128)}, u32[]{:S(2)}) copy-start(f32[4,5,4,4,128]{4,3,2,1,0:T(4,128)} %get-tuple-element.152) | copy-start | bytes 491524
  231.5 5.8 %copy-start.18 = (f32[4,5,4,4,1,128]{5,4,3,2,1,0:T(1,128)S(1)}, f32[4,5,4,4,1,128]{5,4,3,2,1,0:T(1,128)}, u32[]{:S(2)}) copy-start(f32[4,5,4,4,1,128]{5,4,3,2,1,0:T(1,128)} %get-tuple-element.150) | copy-start | bytes 491524
  261.9 29.1 %all-to-all-start.2 = ((f32[4,320,128]{1,0,2:T(4,128)}), f32[4,320,128]{1,0,2:T(4,128)}, u32[]{:S(2)}, u32[]{:S(2)}) async-start(f32[4,320,128]{1,0,2:T(4,128)} %copy.398), calls=%async_computation.2 | async-start | bytes 1572864 | tf_op jit(solution)/shard_map/all_to_all | solution.py:70
  270.7 5.9 %copy-start.5 = (f32[4,5,4,4,1,128]{1,3,2,0,5,4:T(4,128)S(1)}, f32[4,5,4,4,1,128]{1,3,2,0,5,4:T(4,128)}, u32[]{:S(2)}) copy-start(f32[4,5,4,4,1,128]{1,3,2,0,5,4:T(4,128)} %copy.461) | copy-start | bytes 491524
  270.7 7.4 %copy-start.11 = (f32[128,4,5,4,4]{2,4,3,1,0:T(4,128)S(1)}, f32[128,4,5,4,4]{2,4,3,1,0:T(4,128)}, u32[]{:S(2)}) copy-start(f32[128,4,5,4,4]{2,4,3,1,0:T(4,128)} %gather_fusion.10) | copy-start | bytes 491524
  278.1 3.1 copy-start.14
  281.2 4.5 %copy-start.26 = (f32[4,5,1,4,4,64]{5,4,3,1,0,2:T(4,128)S(1)}, f32[4,5,1,4,4,64]{5,4,3,1,0,2:T(4,128)}, u32[]{:S(2)}) copy-start(f32[4,5,1,4,4,64]{5,4,3,1,0,2:T(4,128)} %get-tuple-element.168) | copy-start | bytes 245764
  281.2 4.5 %copy-start.27 = (f32[4,5,1,4,4,64]{5,4,3,1,0,2:T(4,128)S(1)}, f32[4,5,1,4,4,64]{5,4,3,1,0,2:T(4,128)}, u32[]{:S(2)}) copy-start(f32[4,5,1,4,4,64]{5,4,3,1,0,2:T(4,128)} %get-tuple-element.171) | copy-start | bytes 245764
  299.2 36.4 %all-to-all-start.3 = ((f32[32,320,16]{1,2,0:T(8,128)}), f32[32,320,16]{1,2,0:T(8,128)}, u32[]{:S(2)}, u32[]{:S(2)}) async-start(f32[32,320,16]{1,2,0:T(8,128)} %copy.401), calls=%async_computation.3 | async-start | bytes 1572864 | tf_op jit(solution)/shard_map/all_to_all | solution.py:69
  305.1 9.1 %copy-start.2 = (f32[4,5,4,4,128]{1,3,4,2,0:T(4,128)S(1)}, f32[4,5,4,4,128]{1,3,4,2,0:T(4,128)}, u32[]{:S(2)}) copy-start(f32[4,5,4,4,128]{1,3,4,2,0:T(4,128)} %bitcast_subtract_fusion.2) | copy-start | bytes 491524
  305.1 14.7 %copy-start.6 = (f32[4,5,4,4,128]{1,3,2,0,4:T(4,128)S(1)}, f32[4,5,4,4,128]{1,3,2,0,4:T(4,128)}, u32[]{:S(2)}) copy-start(f32[4,5,4,4,128]{1,3,2,0,4:T(4,128)} %bitcast_subtract_fusion.1) | copy-start | bytes 491524
  314.2 13.5 %copy-start.3 = (f32[4,5,4,4,128]{1,3,4,2,0:T(4,128)S(1)}, f32[4,5,4,4,128]{1,3,4,2,0:T(4,128)}, u32[]{:S(2)}) copy-start(f32[4,5,4,4,128]{1,3,4,2,0:T(4,128)} %bitcast_subtract_fusion) | copy-start | bytes 491524
  327.7 12.3 %copy-start.15 = (f32[4,320,128]{2,1,0:T(8,128)S(1)}, f32[4,320,128]{2,1,0:T(8,128)}, u32[]{:S(2)}) copy-start(f32[4,320,128]{2,1,0:T(8,128)} %param.36) | copy-start | bytes 1966084
where the time goes:
time: 349 us; the launch traced here: 344 us
  local copies, waits for them, and re-layouts  162 us (46%)
  matrix products  97.3 us (28%)
  other arithmetic  47.5 us (14%)
  starting transfers between devices  35.7 us (10%)
    dot_general x12, matrix products, face_term(): jnp.einsum('wv,tvabe->twabe', matrix, plus - minus, precision=lax.Precisi...  62.8 us
    unnamed x80, local copies, waits for them, and re-layouts  43.1 us
    sub x10, other arithmetic, face_term(): plus - minus  41.5 us
    gather x2, local copies, waits for them, and re-layouts, space_residual(): jnp.take(high_z, neighbours[2], axis=4)  15.5 us
    gather x2, local copies, waits for them, and re-layouts, space_residual(): jnp.take(low_y, neighbours[1], axis=4)  15.5 us
    gather x2, local copies, waits for them, and re-layouts, space_residual(): jnp.take(low_z, neighbours[3], axis=4)  15.5 us
    gather x2, local copies, waits for them, and re-layouts, space_residual(): jnp.take(high_y, neighbours[0], axis=4)  15.4 us
    all_to_all x2, starting transfers between devices, time_rates(): lax.all_to_all(field, 'inst', split_axis=2, concat_axis=0, tiled=True)  12.1 us
  transfers between devices with their start and end apart: 8, of which 0 were waited for; matrix products, arithmetic and copies ran while one was open for 70% of the time, Pallas kernels for 0%

commit v1 on v0

--- a/solution.py
+++ b/solution.py
@@ -67,7 +67,14 @@
 
 def time_rates(field):
     return lax.all_to_all(
-        differentiate(lax.all_to_all(field, "inst", split_axis=2, concat_axis=0, tiled=True)),
+        differentiate(
+            jnp.concatenate(
+                lax.all_to_all(
+                    jnp.stack(jnp.split(field, lax.axis_size("inst"), axis=2)), "inst", 0, 0
+                ),
+                axis=0,
+            )
+        ),
         "inst",
         split_axis=0,
         concat_axis=2,

time: 349 us -> 387 us (1.11)
  local copies, waits for them, and re-layouts: 162 us -> 198 us
    unnamed x80 -> x103, local copies, waits for them, and re-layouts: 43.1 us -> 68.6 us
    another operation x0 -> x11, local copies, waits for them, and re-layouts: none -> 16.3 us  [time_rates(): jnp.stack(jnp.split(field, lax.axis_size('inst'), axis=2))]
    all_to_all x10 -> x4, local copies, waits for them, and re-layouts: 14.4 us -> 6.71 us  [time_rates(): lax.all_to_all(differentiate(jnp.concatenate(lax.all_to_all(jnp.stack(jnp...]
  transfers between devices with their start and end apart: 8 -> 8, of which waited for: 0 -> 0; matrix products, arithmetic and copies ran while one was open for 70% -> 75% of each run, Pallas kernels for 0% -> 0%
where the time goes in v1:
time: 387 us; the launch traced here: 380 us
  local copies, waits for them, and re-layouts  198 us (51%)
  matrix products  97.5 us (25%)
  other arithmetic  47.4 us (12%)
  starting transfers between devices  35.7 us (9%)
    unnamed x103, local copies, waits for them, and re-layouts  68.6 us
    dot_general x12, matrix products, face_term(): jnp.einsum('wv,tvabe->twabe', matrix, plus - minus, precision=lax.Precisi...  62.7 us
    sub x10, other arithmetic, face_term(): plus - minus  41.4 us
    another operation x11, local copies, waits for them, and re-layouts, time_rates(): jnp.stack(jnp.split(field, lax.axis_size('inst'), axis=2))  16.3 us
    gather x2, local copies, waits for them, and re-layouts, space_residual(): jnp.take(high_y, neighbours[0], axis=4)  15.5 us
    gather x2, local copies, waits for them, and re-layouts, space_residual(): jnp.take(high_z, neighbours[2], axis=4)  15.5 us
    gather x2, local copies, waits for them, and re-layouts, space_residual(): jnp.take(low_z, neighbours[3], axis=4)  15.4 us
    gather x2, local copies, waits for them, and re-layouts, space_residual(): jnp.take(low_y, neighbours[1], axis=4)  15.4 us
  transfers between devices with their start and end apart: 8, of which 0 were waited for; matrix products, arithmetic and copies ran while one was open for 75% of the time, Pallas kernels for 0%

profile of v1, /device:TPU:1, one launch (start us, length us, event | category | flops | bytes accessed | tf_op | source)
XLA Modules:
  0.0 380.0 jit_solution(8829340700310710376)
XLA Ops:
  10.8 4.5 %collective-permute-start = (f32[4,80,64]{1,2,0:T(8,128)}, f32[4,80,64]{1,2,0:T(8,128)S(1)}, u32[]{:S(2)}, u32[]{:S(2)}) collective-permute-start(f32[4,80,64]{1,2,0:T(8,128)} %copy.332), channel_id=1, source_target_pairs={{0,1},{1,2},{2,3},{4,5},{5,6},{6,7},{8,9},{9,10},{10,11},{12,13},{... | collective-permute-start | bytes 245768 | tf_op jit(solution)/shard_map/ppermute | solution.py:22
  15.3 3.4 fusion.289
  28.5 2.0 copy.483
  42.5 6.1 %all-to-all-start = ((f32[8,4,320,16]{2,3,1,0:T(8,128)}), f32[8,4,320,16]{2,3,1,0:T(8,128)}, u32[]{:S(2)}, u32[]{:S(2)}) async-start(f32[8,4,320,16]{2,3,1,0:T(8,128)} %bitcast_dynamic-update-slice_fusion), calls=%async_computation | async-start | bytes 1572864 | tf_op jit(solution)/shard_map/all_to_all | solution.py:72
  48.7 2.2 convolution_bitcast_fusion.5
  50.8 2.0 convolution_bitcast_fusion.4
  56.4 4.4 %copy.477 = f32[4,5,4,4,1,128]{1,3,2,0,5,4:T(4,128)} copy(f32[4,5,4,4,1,128]{5,4,3,2,1,0:T(1,128)} %get-tuple-element.176) | data formatting | bytes 327680
  60.8 4.3 %copy.493 = f32[4,5,4,4,1,128]{1,3,5,2,0,4:T(4,128)} copy(f32[4,5,4,4,1,128]{5,4,3,2,1,0:T(1,128)} %get-tuple-element.176) | data formatting | bytes 327680 | tf_op jit(solution)/shard_map/squeeze | solution.py:125
  65.1 2.4 fusion.145
  67.6 2.4 convolution_add_fusion.3
  72.4 4.6 %copy.473 = f32[4,5,4,1,4,128]{1,4,2,0,5,3:T(4,128)} copy(f32[4,5,4,1,4,128]{5,4,3,2,1,0:T(4,128)} %get-tuple-element.178) | data formatting | bytes 327680
  76.9 4.3 %copy.472 = f32[4,5,4,1,4,128]{1,4,5,2,0,3:T(4,128)} copy(f32[4,5,4,1,4,128]{5,4,3,2,1,0:T(4,128)} %get-tuple-element.179) | data formatting | bytes 327680
  81.3 3.2 copy.350
  84.5 3.3 copy.476
  87.8 7.7 %gather_fusion.2 = f32[128,4,5,4,4]{2,4,3,1,0:T(4,128)} fusion(f32[4,5,4,4,128]{1,3,4,2,0:T(4,128)} %bitcast.472, s32[1024]{0:T(1024)S(1)} %pad_clamp_fusion.3), kind=kCustom, calls=%fused_computation.1.clone | custom fusion | bytes 328192 | tf_op jit(solution)/shard_map/jit(_take)/gather | solution.py:132
  95.5 7.7 %gather_fusion.3 = f32[128,4,5,4,4]{2,4,3,1,0:T(4,128)} fusion(f32[4,5,4,4,128]{1,3,4,2,0:T(4,128)} %copy.350, s32[1024]{0:T(1024)S(1)} %pad_clamp_fusion.2), kind=kCustom, calls=%fused_computation.5.clone | custom fusion | bytes 328192 | tf_op jit(solution)/shard_map/jit(_take)/gather | solution.py:135
  103.2 6.0 %bitcast_subtract_fusion.6 = f32[4,5,4,4,128]{1,3,4,2,0:T(4,128)} fusion(f32[128,4,5,4,4]{2,4,3,1,0:T(4,128)} %gather_fusion.3, pred[128]{0:T(512)(128)(4,1)S(1)} %get-tuple-element.205, f32[4,5,4,1,4,128]{1,4,5,2,0,3:T(4,128)} %copy.472), kind=kLoop, calls=%fused_computation.22 | loop fusion | flops 81920 | bytes 491648 | tf_op jit(solution)/shard_map/sub | solution.py:91
  109.2 7.8 %gather_fusion.4 = f32[128,4,5,4,4]{2,4,3,1,0:T(4,128)} fusion(f32[4,5,4,4,128]{1,3,4,2,0:T(4,128)} %bitcast.473, s32[1024]{0:T(1024)S(1)} %pad_clamp_fusion.1), kind=kCustom, calls=%fused_computation.6.clone | custom fusion | bytes 328192 | tf_op jit(solution)/shard_map/jit(_take)/gather | solution.py:138
  116.9 7.7 %gather_fusion.5 = f32[128,4,5,4,4]{2,4,3,1,0:T(4,128)} fusion(f32[4,5,4,4,128]{1,3,4,2,0:T(4,128)} %bitcast.477, s32[1024]{0:T(1024)S(1)} %pad_clamp_fusion), kind=kCustom, calls=%fused_computation.7.clone | custom fusion | bytes 328192 | tf_op jit(solution)/shard_map/jit(_take)/gather | solution.py:141
  124.6 5.9 %bitcast_subtract_fusion.4 = f32[4,5,4,4,128]{1,3,4,2,0:T(4,128)} fusion(f32[128,4,5,4,4]{2,4,3,1,0:T(4,128)} %gather_fusion.5, pred[128]{0:T(512)(128)(4,1)S(1)} %get-tuple-element.203, f32[4,5,4,4,1,128]{1,3,5,2,0,4:T(4,128)} %copy.476), kind=kLoop, calls=%fused_computation.20 | loop fusion | flops 81920 | bytes 491648 | tf_op jit(solution)/shard_map/sub | solution.py:91
  132.1 3.1 bitcast_subtract_fusion.7
  137.1 3.5 bitcast_subtract_fusion.5
  150.0 6.9 %fusion.126 = f32[4,5,4,4,4,128]{5,1,4,3,2,0:T(8,128)} fusion(f32[4,5,4,4,4,128]{5,1,4,3,2,0:T(8,128)} %fusion.134, f32[4,5,4,1,4,128]{5,1,4,2,0,3:T(8,128)S(1)} %slice_bitcast_fusion.10, f32[4,5,4,4,128]{1,3,2,0,4:T(4,128)S(1)} %copy-done.8, f32[1,5,5]{2,0,1:T(1,128)S(1)} %get-tuple-element.193), kind=kOutput, calls=%fused_computation.98 | convolution fusion | flops 2539620 | bytes 589924 | tf_op jit(solution)/shard_map/wv,tvabe->twabe/dot_general | solution.py:91
  158.6 2.1 fusion.149
  162.1 5.6 %all-to-all-start.1 = ((f32[32,320,16]{1,2,0:T(8,128)}), f32[32,320,16]{1,2,0:T(8,128)S(1)}, u32[]{:S(2)}, u32[]{:S(2)}) async-start(f32[32,320,16]{1,2,0:T(8,128)} %copy.372), calls=%async_computation.1 | async-start | bytes 1572864 | tf_op jit(solution)/shard_map/all_to_all | solution.py:69
  167.7 6.8 %fusion.117 = f32[4,5,4,4,4,128]{5,1,4,3,2,0:T(8,128)} fusion(f32[4,5,4,4,4,128]{5,1,4,3,2,0:T(8,128)} %fusion.126, f32[4,5,4,1,4,128]{5,1,4,2,0,3:T(8,128)} %slice_bitcast_fusion.9, f32[4,5,4,4,128]{1,3,4,2,0:T(4,128)} %bitcast_subtract_fusion.6, f32[1,5,5]{2,0,1:T(1,128)S(1)} %get-tuple-element.193), kind=kOutput, calls=%fused_computation.95 | convolution fusion | flops 2539595 | bytes 4718692 | tf_op jit(solution)/shard_map/wv,tvabe->twabe/dot_general | solution.py:91
  175.5 8.9 %fusion.108 = f32[4,5,4,4,4,128]{5,1,4,3,2,0:T(8,128)} fusion(f32[4,5,4,4,4,128]{5,1,4,3,2,0:T(8,128)} %fusion.117, f32[4,5,4,4,1,128]{5,1,3,2,0,4:T(8,128)S(1)} %slice_bitcast_fusion.8, f32[4,5,4,4,128]{1,3,2,0,4:T(4,128)} %bitcast_subtract_fusion.5, f32[1,5,5]{2,0,1:T(1,128)S(1)} %get-tuple-element.192), kind=kOutput, calls=%fused_computation.92 | convolution fusion | flops 2539620 | bytes 4620388 | tf_op jit(solution)/shard_map/wv,tvabe->twabe/dot_general | solution.py:91
  184.4 5.7 %fusion.99 = f32[4,5,4,4,4,128]{5,1,4,3,2,0:T(8,128)} fusion(f32[4,5,4,4,4,128]{5,1,4,3,2,0:T(8,128)} %fusion.108, f32[4,5,4,4,128]{1,3,4,2,0:T(4,128)S(1)} %copy-done.5, f32[1,5,5]{2,0,1:T(1,128)S(1)} %get-tuple-element.192), kind=kOutput, calls=%fused_computation.89 | convolution fusion | flops 2539595 | bytes 688228 | tf_op jit(solution)/shard_map/wv,tvabe->twabe/dot_general | solution.py:91
  190.1 2.2 copy.362
  199.4 2.1 convolution_bitcast_fusion.1
  201.5 2.1 convolution_bitcast_fusion
  206.1 3.3 copy.491
  209.4 3.1 copy.495
  212.5 3.5 slice_bitcast_fusion
  216.0 2.3 fusion.141
  223.6 2.1 collective-permute-start.3
  227.2 3.7 collective-permute-start.2
  230.9 3.8 %copy.489 = f32[4,5,4,1,4,128]{1,4,2,0,5,3:T(4,128)} copy(f32[4,5,4,1,4,128]{5,4,3,2,1,0:T(4,128)S(1)} %copy-done.24) | data formatting | bytes 327680
  234.7 3.2 copy.488
  237.9 7.8 %gather_fusion.8 = f32[128,4,5,4,4]{2,4,3,1,0:T(4,128)} fusion(f32[4,5,4,4,128]{1,3,4,2,0:T(4,128)} %bitcast.474, s32[1024]{0:T(1024)S(1)} %pad_clamp_fusion.3), kind=kCustom, calls=%fused_computation.8.clone | custom fusion | bytes 328192 | tf_op jit(solution)/shard_map/jit(_take)/gather | solution.py:132
  245.7 3.1 copy.400
  248.8 7.7 %gather_fusion.9 = f32[128,4,5,4,4]{2,4,3,1,0:T(4,128)} fusion(f32[4,5,4,4,128]{1,3,4,2,0:T(4,128)} %copy.400, s32[1024]{0:T(1024)S(1)} %pad_clamp_fusion.2), kind=kCustom, calls=%fused_computation.9.clone | custom fusion | bytes 328192 | tf_op jit(solution)/shard_map/jit(_take)/gather | solution.py:135
  256.5 5.8 %bitcast_subtract_fusion.2 = f32[4,5,4,4,128]{1,3,4,2,0:T(4,128)} fusion(f32[128,4,5,4,4]{2,4,3,1,0:T(4,128)} %gather_fusion.9, pred[128]{0:T(512)(128)(4,1)S(1)} %get-tuple-element.205, f32[4,5,4,1,4,128]{1,4,5,2,0,3:T(4,128)} %copy.488), kind=kLoop, calls=%fused_computation.16 | loop fusion | flops 81920 | bytes 491648 | tf_op jit(solution)/shard_map/sub | solution.py:91
  262.3 3.3 copy.490
  265.5 7.7 %gather_fusion.10 = f32[128,4,5,4,4]{2,4,3,1,0:T(4,128)} fusion(f32[4,5,4,4,128]{1,3,4,2,0:T(4,128)} %bitcast.475, s32[1024]{0:T(1024)S(1)} %pad_clamp_fusion.1), kind=kCustom, calls=%fused_computation.10.clone | custom fusion | bytes 328192 | tf_op jit(solution)/shard_map/jit(_take)/gather | solution.py:138
  273.2 7.7 %gather_fusion.11 = f32[128,4,5,4,4]{2,4,3,1,0:T(4,128)} fusion(f32[4,5,4,4,128]{1,3,4,2,0:T(4,128)} %bitcast.476, s32[1024]{0:T(1024)S(1)} %pad_clamp_fusion), kind=kCustom, calls=%fused_computation.11.clone | custom fusion | bytes 328192 | tf_op jit(solution)/shard_map/jit(_take)/gather | solution.py:141
  281.0 5.8 %bitcast_subtract_fusion = f32[4,5,4,4,128]{1,3,4,2,0:T(4,128)} fusion(f32[128,4,5,4,4]{2,4,3,1,0:T(4,128)} %gather_fusion.11, pred[128]{0:T(512)(128)(4,1)S(1)} %get-tuple-element.203, f32[4,5,4,4,1,128]{1,3,5,2,0,4:T(4,128)} %copy.490), kind=kLoop, calls=%fused_computation.12 | loop fusion | flops 81920 | bytes 491648 | tf_op jit(solution)/shard_map/sub | solution.py:91
  302.5 6.0 %all-to-all-start.2 = ((f32[8,4,320,16]{2,3,1,0:T(8,128)}), f32[8,4,320,16]{2,3,1,0:T(8,128)}, u32[]{:S(2)}, u32[]{:S(2)}) async-start(f32[8,4,320,16]{2,3,1,0:T(8,128)} %constant_dynamic-update-slice_fusion), calls=%async_computation.2 | async-start | bytes 1572864 | tf_op jit(solution)/shard_map/all_to_all | solution.py:72
  308.5 2.8 convolution_add_fusion.1
  311.3 5.8 %bitcast_subtract_fusion.3 = f32[4,5,4,4,128]{1,3,2,0,4:T(4,128)} fusion(f32[4,5,4,1,4,128]{1,4,2,0,5,3:T(4,128)} %copy.489, f32[128,4,5,4,4]{2,4,3,1,0:T(4,128)} %gather_fusion.8, pred[128]{0:T(512)(128)(4,1)S(1)} %get-tuple-element.206), kind=kLoop, calls=%fused_computation.19 | loop fusion | flops 81920 | bytes 491648 | tf_op jit(solution)/shard_map/sub | solution.py:91
  318.7 3.1 bitcast_subtract_fusion.1
  321.8 2.3 fusion.16
  327.4 2.1 fusion.136
  329.4 2.1 fusion.138
  331.5 2.1 fusion.147
  335.0 5.8 %all-to-all-start.3 = ((f32[32,320,16]{1,2,0:T(8,128)}), f32[32,320,16]{1,2,0:T(8,128)}, u32[]{:S(2)}, u32[]{:S(2)}) async-start(f32[32,320,16]{1,2,0:T(8,128)} %copy.421), calls=%async_computation.3 | async-start | bytes 1572864 | tf_op jit(solution)/shard_map/all_to_all | solution.py:69
  340.8 9.1 %fusion.81 = f32[4,5,4,4,4,128]{5,1,3,2,0,4:T(8,128)} fusion(f32[4,5,4,4,4,128]{5,1,3,2,0,4:T(8,128)} %fusion.138, f32[4,5,4,4,128]{1,3,2,0,4:T(4,128)} %bitcast_subtract_fusion.3, f32[1,5,5]{2,0,1:T(1,128)S(1)} %get-tuple-element.193), kind=kOutput, calls=%fused_computation.83 | convolution fusion | flops 2539620 | bytes 4718692 | tf_op jit(solution)/shard_map/wv,tvabe->twabe/dot_general | solution.py:91
  349.9 5.6 %fusion.75 = f32[4,5,4,4,4,128]{5,1,3,2,0,4:T(8,128)} fusion(f32[4,5,4,4,4,128]{5,1,3,2,0,4:T(8,128)} %fusion.81, f32[4,5,4,4,128]{1,3,4,2,0:T(4,128)S(1)} %copy-done.2, f32[1,5,5]{2,0,1:T(1,128)S(1)} %get-tuple-element.193), kind=kOutput, calls=%fused_computation.81 | convolution fusion | flops 2539595 | bytes 688228 | tf_op jit(solution)/shard_map/wv,tvabe->twabe/dot_general | solution.py:91
  355.5 7.9 %fusion.93 = f32[4,5,4,4,4,128]{5,1,3,2,0,4:T(8,128)} fusion(f32[4,5,4,4,4,128]{5,1,3,2,0,4:T(8,128)} %fusion.75, f32[4,5,4,4,128]{1,3,2,0,4:T(4,128)S(1)} %copy-done.6, f32[1,5,5]{2,0,1:T(1,128)S(1)} %get-tuple-element.192), kind=kOutput, calls=%fused_computation.87 | convolution fusion | flops 2539620 | bytes 688228 | tf_op jit(solution)/shard_map/wv,tvabe->twabe/dot_general | solution.py:91
  363.4 5.5 %fusion.87 = f32[4,5,4,4,4,128]{5,1,3,2,0,4:T(8,128)} fusion(f32[4,5,4,4,4,128]{5,1,3,2,0,4:T(8,128)} %fusion.93, f32[4,5,4,4,128]{1,3,4,2,0:T(4,128)S(1)} %copy-done.4, f32[1,5,5]{2,0,1:T(1,128)S(1)} %get-tuple-element.192), kind=kOutput, calls=%fused_computation.85 | convolution fusion | flops 2539595 | bytes 688228 | tf_op jit(solution)/shard_map/wv,tvabe->twabe/dot_general | solution.py:91
  368.9 2.5 copy.411
  371.5 2.1 copy.422
  373.6 2.2 copy.423
  375.8 4.0 %fusion.18 = f32[4,320,128]{2,1,0:T(8,128)} fusion(f32[4,320,128]{2,1,0:T(8,128)S(1)} %fusion.19, f32[4,320,320]{2,1,0:T(8,128)S(1)} %copy-done, f32[4,320,128]{2,1,0:T(8,128)S(1)} %copy-done.15, f32[4,320,128]{2,1,0:T(8,128)} %bitcast.481, f32[4,320,128]{2,1,0:T(8,128)} %copy.423), kind=kOutput, calls=%fused_computation.53 | convolution fusion | flops 629637120 | bytes 4915200 | tf_op jit(solution)/shard_map/tpq,tqe->tpe/dot_general | solution.py:164
  (178 shorter events, 92.8 us)
Async XLA Ops:
  0.6 195.5 %copy-start = (f32[4,320,320]{2,1,0:T(8,128)S(1)}, f32[4,320,320]{2,1,0:T(8,128)}, u32[]{:S(2)}) copy-start(f32[4,320,320]{2,1,0:T(8,128)} %param.38) | copy-start | bytes 4915204
  0.6 14.7 %copy-start.1 = (f32[4,320,128]{2,1,0:T(8,128)S(1)}, f32[4,320,128]{2,1,0:T(8,128)}, u32[]{:S(2)}) copy-start(f32[4,320,128]{2,1,0:T(8,128)} %param.35) | copy-start | bytes 1966084
  7.4 137.0 %collective-permute-start.1 = (f32[4,80,64]{2,1,0:T(8,128)}, f32[4,80,64]{2,1,0:T(8,128)}, u32[]{:S(2)}, u32[]{:S(2)}) collective-permute-start(f32[4,80,64]{2,1,0:T(8,128)} %select_bitcast_fusion.1), channel_id=1, source_target_pairs={{1,0},{2,1},{3,2},{5,4},{6,5},{7,6},{9,8},{10,9},{11,10},{13,12},{... | collective-permute-start | bytes 245768 | tf_op jit(solution)/shard_map/ppermute | solution.py:25
  10.8 129.8 %collective-permute-start = (f32[4,80,64]{1,2,0:T(8,128)}, f32[4,80,64]{1,2,0:T(8,128)S(1)}, u32[]{:S(2)}, u32[]{:S(2)}) collective-permute-start(f32[4,80,64]{1,2,0:T(8,128)} %copy.332), channel_id=1, source_target_pairs={{0,1},{1,2},{2,3},{4,5},{5,6},{6,7},{8,9},{9,10},{10,11},{12,13},{... | collective-permute-start | bytes 245768 | tf_op jit(solution)/shard_map/ppermute | solution.py:22
  20.0 28.7 %copy-start.29 = (f32[4,4,1,1,1,1]{1,0,5,4,3,2:T(4,128)S(1)}, f32[4,4,1,1,1,1]{1,0,5,4,3,2:T(4,128)}, u32[]{:S(2)}) copy-start(f32[4,4,1,1,1,1]{1,0,5,4,3,2:T(4,128)} %constant.421) | copy-start | bytes 196
  30.5 23.6 %copy-start.30 = (s32[4,1,64]{2,1,0:T(1,128)S(1)}, s32[4,1,64]{2,1,0:T(1,128)}, u32[]{:S(2)}) copy-start(s32[4,1,64]{2,1,0:T(1,128)} %param.40) | copy-start | bytes 3076
  31.8 23.1 %copy-start.32 = (s32[4,64]{1,0:T(4,128)S(1)}, s32[4,64]{1,0:T(4,128)}, u32[]{:S(2)}) copy-start(s32[4,64]{1,0:T(4,128)} %param.39) | copy-start | bytes 3076
  42.5 116.1 %all-to-all-start = ((f32[8,4,320,16]{2,3,1,0:T(8,128)}), f32[8,4,320,16]{2,3,1,0:T(8,128)}, u32[]{:S(2)}, u32[]{:S(2)}) async-start(f32[8,4,320,16]{2,3,1,0:T(8,128)} %bitcast_dynamic-update-slice_fusion), calls=%async_computation | async-start | bytes 1572864 | tf_op jit(solution)/shard_map/all_to_all | solution.py:72
  56.4 8.7 %copy-start.31 = (f32[3,5,5]{2,0,1:T(4,128)S(1)}, f32[3,5,5]{2,0,1:T(4,128)}, u32[]{:S(2)}) copy-start(f32[3,5,5]{2,0,1:T(4,128)} %param.37) | copy-start | bytes 904
  71.4 1.0 copy-start.10
  72.4 8.9 %copy-start.21 = (f32[4,5,4,4,128]{4,3,2,1,0:T(4,128)S(1)}, f32[4,5,4,4,128]{4,3,2,1,0:T(4,128)}, u32[]{:S(2)}) copy-start(f32[4,5,4,4,128]{4,3,2,1,0:T(4,128)} %get-tuple-element.177) | copy-start | bytes 491524
  76.9 7.5 %copy-start.20 = (f32[4,5,4,4,1,128]{5,4,3,2,1,0:T(1,128)S(1)}, f32[4,5,4,4,1,128]{5,4,3,2,1,0:T(1,128)}, u32[]{:S(2)}) copy-start(f32[4,5,4,4,1,128]{5,4,3,2,1,0:T(1,128)} %get-tuple-element.175) | copy-start | bytes 491524
  124.6 5.9 %copy-start.9 = (f32[4,5,4,1,4,128]{1,4,2,0,5,3:T(4,128)S(1)}, f32[4,5,4,1,4,128]{1,4,2,0,5,3:T(4,128)}, u32[]{:S(2)}) copy-start(f32[4,5,4,1,4,128]{1,4,2,0,5,3:T(4,128)} %copy.473) | copy-start | bytes 491524
  124.6 7.4 %copy-start.12 = (f32[128,4,5,4,4]{2,4,3,1,0:T(4,128)S(1)}, f32[128,4,5,4,4]{2,4,3,1,0:T(4,128)}, u32[]{:S(2)}) copy-start(f32[128,4,5,4,4]{2,4,3,1,0:T(4,128)} %gather_fusion.2) | copy-start | bytes 491524
  132.1 3.1 copy-start.7
  132.1 5.0 %copy-start.13 = (f32[128,4,5,4,4]{2,4,3,1,0:T(4,128)S(1)}, f32[128,4,5,4,4]{2,4,3,1,0:T(4,128)}, u32[]{:S(2)}) copy-start(f32[128,4,5,4,4]{2,4,3,1,0:T(4,128)} %gather_fusion.4) | copy-start | bytes 491524
  137.1 7.4 %copy-start.25 = (f32[4,5,1,4,4,64]{5,4,3,1,0,2:T(4,128)S(1)}, f32[4,5,1,4,4,64]{5,4,3,1,0,2:T(4,128)}, u32[]{:S(2)}) copy-start(f32[4,5,1,4,4,64]{5,4,3,1,0,2:T(4,128)} %get-tuple-element.188) | copy-start | bytes 245764
  137.1 7.4 %copy-start.26 = (f32[4,5,1,4,4,64]{5,4,3,1,0,2:T(4,128)S(1)}, f32[4,5,1,4,4,64]{5,4,3,1,0,2:T(4,128)}, u32[]{:S(2)}) copy-start(f32[4,5,1,4,4,64]{5,4,3,1,0,2:T(4,128)} %get-tuple-element.191) | copy-start | bytes 245764
  143.3 6.7 %copy-start.8 = (f32[4,5,4,4,128]{1,3,2,0,4:T(4,128)S(1)}, f32[4,5,4,4,128]{1,3,2,0,4:T(4,128)}, u32[]{:S(2)}) copy-start(f32[4,5,4,4,128]{1,3,2,0,4:T(4,128)} %bitcast_subtract_fusion.7) | copy-start | bytes 491524
  162.1 30.2 %all-to-all-start.1 = ((f32[32,320,16]{1,2,0:T(8,128)}), f32[32,320,16]{1,2,0:T(8,128)S(1)}, u32[]{:S(2)}, u32[]{:S(2)}) async-start(f32[32,320,16]{1,2,0:T(8,128)} %copy.372), calls=%async_computation.1 | async-start | bytes 1572864 | tf_op jit(solution)/shard_map/all_to_all | solution.py:69
  167.7 16.7 %copy-start.5 = (f32[4,5,4,4,128]{1,3,4,2,0:T(4,128)S(1)}, f32[4,5,4,4,128]{1,3,4,2,0:T(4,128)}, u32[]{:S(2)}) copy-start(f32[4,5,4,4,128]{1,3,4,2,0:T(4,128)} %bitcast_subtract_fusion.4) | copy-start | bytes 491524
  196.1 8.2 %copy-start.16 = (f32[4,320,128]{2,1,0:T(8,128)}, f32[4,320,128]{2,1,0:T(8,128)S(1)}, u32[]{:S(2)}) copy-start(f32[4,320,128]{2,1,0:T(8,128)S(1)} %add_subtract_fusion) | copy-start | bytes 1966084
  212.5 5.9 %copy-start.18 = (f32[4,5,4,4,128]{4,3,2,1,0:T(4,128)S(1)}, f32[4,5,4,4,128]{4,3,2,1,0:T(4,128)}, u32[]{:S(2)}) copy-start(f32[4,5,4,4,128]{4,3,2,1,0:T(4,128)} %get-tuple-element.165) | copy-start | bytes 491524
  216.0 9.7 %copy-start.17 = (f32[4,5,4,4,128]{4,3,2,1,0:T(4,128)S(1)}, f32[4,5,4,4,128]{4,3,2,1,0:T(4,128)}, u32[]{:S(2)}) copy-start(f32[4,5,4,4,128]{4,3,2,1,0:T(4,128)} %get-tuple-element.166) | copy-start | bytes 491524
  218.4 12.5 %copy-start.24 = (f32[4,5,4,1,4,128]{5,4,3,2,1,0:T(4,128)S(1)}, f32[4,5,4,1,4,128]{5,4,3,2,1,0:T(4,128)}, u32[]{:S(2)}) copy-start(f32[4,5,4,1,4,128]{5,4,3,2,1,0:T(4,128)} %get-tuple-element.161) | copy-start | bytes 491524
  218.4 16.3 %copy-start.23 = (f32[4,5,4,1,4,128]{5,4,3,2,1,0:T(4,128)S(1)}, f32[4,5,4,1,4,128]{5,4,3,2,1,0:T(4,128)}, u32[]{:S(2)}) copy-start(f32[4,5,4,1,4,128]{5,4,3,2,1,0:T(4,128)} %get-tuple-element.162) | copy-start | bytes 491524
  223.6 102.6 %collective-permute-start.3 = (f32[4,80,64]{2,1,0:T(8,128)}, f32[4,80,64]{2,1,0:T(8,128)}, u32[]{:S(2)}, u32[]{:S(2)}) collective-permute-start(f32[4,80,64]{2,1,0:T(8,128)} %select_bitcast_fusion), channel_id=1, source_target_pairs={{1,0},{2,1},{3,2},{5,4},{6,5},{7,6},{9,8},{10,9},{11,10},{13,12},{... | collective-permute-start | bytes 245768 | tf_op jit(solution)/shard_map/ppermute | solution.py:25
  227.2 96.9 %collective-permute-start.2 = (f32[4,80,64]{1,2,0:T(8,128)}, f32[4,80,64]{1,2,0:T(8,128)S(1)}, u32[]{:S(2)}, u32[]{:S(2)}) collective-permute-start(f32[4,80,64]{1,2,0:T(8,128)} %copy.384), channel_id=1, source_target_pairs={{0,1},{1,2},{2,3},{4,5},{5,6},{6,7},{8,9},{9,10},{10,11},{12,13},{... | collective-permute-start | bytes 245768 | tf_op jit(solution)/shard_map/ppermute | solution.py:22
  230.8 14.8 %copy-start.22 = (f32[4,5,4,4,128]{4,3,2,1,0:T(4,128)S(1)}, f32[4,5,4,4,128]{4,3,2,1,0:T(4,128)}, u32[]{:S(2)}) copy-start(f32[4,5,4,4,128]{4,3,2,1,0:T(4,128)} %get-tuple-element.160) | copy-start | bytes 491524
  256.5 5.8 %copy-start.19 = (f32[4,5,4,4,1,128]{5,4,3,2,1,0:T(1,128)S(1)}, f32[4,5,4,4,1,128]{5,4,3,2,1,0:T(1,128)}, u32[]{:S(2)}) copy-start(f32[4,5,4,4,1,128]{5,4,3,2,1,0:T(1,128)} %get-tuple-element.158) | copy-start | bytes 491524
  302.5 29.0 %all-to-all-start.2 = ((f32[8,4,320,16]{2,3,1,0:T(8,128)}), f32[8,4,320,16]{2,3,1,0:T(8,128)}, u32[]{:S(2)}, u32[]{:S(2)}) async-start(f32[8,4,320,16]{2,3,1,0:T(8,128)} %constant_dynamic-update-slice_fusion), calls=%async_computation.2 | async-start | bytes 1572864 | tf_op jit(solution)/shard_map/all_to_all | solution.py:72
  311.2 5.8 %copy-start.3 = (f32[4,5,4,4,1,128]{1,3,2,0,5,4:T(4,128)S(1)}, f32[4,5,4,4,1,128]{1,3,2,0,5,4:T(4,128)}, u32[]{:S(2)}) copy-start(f32[4,5,4,4,1,128]{1,3,2,0,5,4:T(4,128)} %copy.491) | copy-start | bytes 491524
  311.3 7.4 %copy-start.11 = (f32[128,4,5,4,4]{2,4,3,1,0:T(4,128)S(1)}, f32[128,4,5,4,4]{2,4,3,1,0:T(4,128)}, u32[]{:S(2)}) copy-start(f32[128,4,5,4,4]{2,4,3,1,0:T(4,128)} %gather_fusion.10) | copy-start | bytes 491524
  318.7 3.1 copy-start.14
  321.8 4.4 %copy-start.27 = (f32[4,5,1,4,4,64]{5,4,3,1,0,2:T(4,128)S(1)}, f32[4,5,1,4,4,64]{5,4,3,1,0,2:T(4,128)}, u32[]{:S(2)}) copy-start(f32[4,5,1,4,4,64]{5,4,3,1,0,2:T(4,128)} %get-tuple-element.184) | copy-start | bytes 245764
  321.8 4.4 %copy-start.28 = (f32[4,5,1,4,4,64]{5,4,3,1,0,2:T(4,128)S(1)}, f32[4,5,1,4,4,64]{5,4,3,1,0,2:T(4,128)}, u32[]{:S(2)}) copy-start(f32[4,5,1,4,4,64]{5,4,3,1,0,2:T(4,128)} %get-tuple-element.187) | copy-start | bytes 245764
  335.0 36.5 %all-to-all-start.3 = ((f32[32,320,16]{1,2,0:T(8,128)}), f32[32,320,16]{1,2,0:T(8,128)}, u32[]{:S(2)}, u32[]{:S(2)}) async-start(f32[32,320,16]{1,2,0:T(8,128)} %copy.421), calls=%async_computation.3 | async-start | bytes 1572864 | tf_op jit(solution)/shard_map/all_to_all | solution.py:69
  340.8 9.1 %copy-start.2 = (f32[4,5,4,4,128]{1,3,4,2,0:T(4,128)S(1)}, f32[4,5,4,4,128]{1,3,4,2,0:T(4,128)}, u32[]{:S(2)}) copy-start(f32[4,5,4,4,128]{1,3,4,2,0:T(4,128)} %bitcast_subtract_fusion.2) | copy-start | bytes 491524
  340.8 14.7 %copy-start.6 = (f32[4,5,4,4,128]{1,3,2,0,4:T(4,128)S(1)}, f32[4,5,4,4,128]{1,3,2,0,4:T(4,128)}, u32[]{:S(2)}) copy-start(f32[4,5,4,4,128]{1,3,2,0,4:T(4,128)} %bitcast_subtract_fusion.1) | copy-start | bytes 491524
  349.9 13.5 %copy-start.4 = (f32[4,5,4,4,128]{1,3,4,2,0:T(4,128)S(1)}, f32[4,5,4,4,128]{1,3,4,2,0:T(4,128)}, u32[]{:S(2)}) copy-start(f32[4,5,4,4,128]{1,3,4,2,0:T(4,128)} %bitcast_subtract_fusion) | copy-start | bytes 491524
  363.4 12.4 %copy-start.15 = (f32[4,320,128]{2,1,0:T(8,128)S(1)}, f32[4,320,128]{2,1,0:T(8,128)}, u32[]{:S(2)}) copy-start(f32[4,320,128]{2,1,0:T(8,128)} %param.36) | copy-start | bytes 1966084
